TPU v7x, 32 devices: a whole 2x2x4 slice. The times are simulated.
32 devices in a mesh: grp: 4 (over y, x), dev: 8 (over z, core).
Axes of the slice: x: 2, y: 2, z: 4, core: 2. Of those that a mesh axis runs over, the one named last changes fastest.
Arguments:
- particles: float32 [128, 5, 128], P(('grp', 'dev')), as said below
- entropy: float32 [128, 128], P(('grp', 'dev')), may hold values from 0.5 to 2
- lists: int32 [128, 64], P(('grp', 'dev')), may hold values from 0 to 127, as said below
- counts: int32 [128], P(('grp', 'dev')), may hold values from 16 to 64, as said below
Outputs:
- density: float32 [128, 128], P(('grp', 'dev'))
- accel: float32 [128, 3, 128], P(('grp', 'dev'))
Inputs may be any that keep to these rules, and one draw needn't show every extreme that they name: lists[c, 0] = c; every id lies in the group of c or in one of the two groups next to it, counting groups of 32 cells around a loop. `counts`: each count is a multiple of 16. `particles`: coordinates in 0 to 1 within the group's slab, masses positive, smoothing lengths from 0.3 to 0.6.
All inputs are finite; a program needn't handle non-finite values.
Results may differ from a plain program's by a relative error of at most 0.0003.
Values sent between devices are 32-bit elements; how exact they have to be, the bound alone decides.
No kernel may reach another device: no remote copies, remote signals or barrier semaphores. Data moves between devices by JAX's collectives and lax.ppermute only.
A program may use at most 64 MiB of HBM per device.

v0:
```python
import math
import jax
import jax.numpy as jnp
from jax import lax
from jax.sharding import PartitionSpec as P

NB = 64
NBLK = 8
norm_const = 21.0 / (16.0 * math.pi)


def padded(block, sides, width):
    for axis, dim in sides:
        count = lax.axis_size(axis)
        forward = [(i, i + 1) for i in range(count - 1)]
        forward.append((count - 1, 0))
        backward = [(target, source) for source, target in forward]
        low = lax.ppermute(
            lax.slice_in_dim(block, block.shape[dim] - width, None, axis=dim), axis, forward
        )
        high = lax.ppermute(lax.slice_in_dim(block, 0, width, axis=dim), axis, backward)
        block = jnp.concatenate([low, block, high], axis=dim)
    return block


def kernel_parts(dist_sq, smooth):
    ratio = jnp.sqrt(dist_sq) / smooth
    base_of = jnp.maximum(1.0 - 0.5 * ratio, 0.0)
    kernel = norm_const / smooth**3 * base_of**4 * (1.0 + 2.0 * ratio)
    slope = -5.0 * norm_const / smooth**5 * base_of**3
    return (kernel, slope)


def on_device(particles, entropy, lists, counts):
    own_cells = particles.shape[0]
    groups = lax.axis_size("grp")
    members = lax.axis_size("dev")
    group_cells = own_cells * members
    group_at = lax.axis_index("grp")
    group_of = lists // group_cells
    within = lists % group_cells
    side_of = (group_of - group_at + 1 + groups) % groups
    shift_all = (side_of - 1).astype(jnp.float32)
    member_of = within // own_cells
    cell_of = within % own_cells
    rimmed = padded(particles, (("grp", 0),), own_cells)
    extended = lax.all_gather(rimmed, "dev", axis=0, tiled=True)
    slots_ext = member_of * (3 * own_cells) + side_of * own_cells + cell_of
    upper = NB // NBLK
    slot_range = jnp.arange(NBLK, dtype=jnp.int32)
    own_smooth = particles[:, None, 4, :, None]
    unit_first = jnp.array([1.0, 0.0, 0.0], dtype=jnp.float32)

    def fetch_block(block_at):
        chosen = lax.dynamic_slice_in_dim(slots_ext, block_at * NBLK, NBLK, 1)
        shift_blk = lax.dynamic_slice_in_dim(shift_all, block_at * NBLK, NBLK, 1)
        others = extended[chosen]
        live = ((block_at * NBLK + slot_range)[None, :] < counts[:, None]).astype(jnp.float32)
        offset = particles[:, None, :3, :, None] - others[:, :, :3, None, :]
        offset = offset - shift_blk[:, :, None, None, None] * unit_first[None, None, :, None, None]
        dist_sq = jnp.sum(offset * offset, axis=2)
        return (chosen, others, live, offset, dist_sq)

    def density_step(block_at, total):
        chosen, others, live, offset, dist_sq = fetch_block(block_at)
        kernel, slope = kernel_parts(dist_sq, own_smooth)
        return total + jnp.sum(
            live[:, :, None, None] * others[:, :, 3, None, :] * kernel, axis=(1, 3)
        )

    density = lax.fori_loop(
        0, upper, density_step, jnp.zeros((own_cells, particles.shape[2]), jnp.float32)
    )
    pressure = entropy * density ** (5.0 / 3.0)
    weight = pressure / (density * density)
    weight_rim = padded(weight, (("grp", 0),), own_cells)
    weight_ext = lax.all_gather(weight_rim, "dev", axis=0, tiled=True)

    def force_step(block_at, total):
        chosen, others, live, offset, dist_sq = fetch_block(block_at)
        kernel_i, slope_i = kernel_parts(dist_sq, own_smooth)
        kernel_j, slope_j = kernel_parts(dist_sq, others[:, :, 4, None, :])
        factor = (
            live[:, :, None, None]
            * others[:, :, 3, None, :]
            * (weight[:, None, :, None] * slope_i + weight_ext[chosen][:, :, None, :] * slope_j)
        )
        return total - jnp.sum(factor[:, :, None] * offset, axis=(1, 4))

    accel = lax.fori_loop(
        0, upper, force_step, jnp.zeros((own_cells, 3, particles.shape[2]), jnp.float32)
    )
    return (density, accel)


def solution(mesh):
    return jax.shard_map(
        on_device,
        mesh=mesh,
        in_specs=(
            P(("grp", "dev"), None, None),
            P(("grp", "dev"), None),
            P(("grp", "dev"), None),
            P(("grp", "dev")),
        ),
        out_specs=(P(("grp", "dev"), None), P(("grp", "dev"), None, None)),
        check_vma=False,
    )
```

profile of v0, /device:TPU:0, one launch (start us, length us, event | category | flops | bytes accessed | tf_op | source)
XLA Modules:
  0.0 148.0 jit_solution(8237750292582553730)
XLA Ops:
  1.3 3.9 %collective-permute-start.1 = (f32[4,5,128]{2,1,0:T(8,128)S(1)}, f32[4,5,128]{2,1,0:T(8,128)S(1)}, u32[]{:S(2)}, u32[]{:S(2)}) collective-permute-start(f32[4,5,128]{2,1,0:T(8,128)S(1)} %copy.28), channel_id=1, source_target_pairs={{8,0},{16,8},{24,16},{0,24},{9,1},{17,9},{25,17},{1,25},{10,2},{18... | collective-permute-start | bytes 30728 | tf_op jit(solution)/shard_map/ppermute | solution.py:21
  8.0 1.9 %collective-permute-done = f32[4,5,128]{2,1,0:T(8,128)S(1)} collective-permute-done((f32[4,5,128]{2,1,0:T(8,128)S(1)}, f32[4,5,128]{2,1,0:T(8,128)S(1)}, u32[]{:S(2)}, u32[]{:S(2)}) %collective-permute-start) | collective-permute-done | bytes 10272 | tf_op jit(solution)/shard_map/ppermute | solution.py:18
  9.9 14.7 %all_gather.6 = f32[96,5,128]{2,1,0:T(8,128)S(1)} all-gather(f32[12,5,128]{2,1,0:T(8,128)S(1)} %pad_maximum_fusion), channel_id=1, replica_groups=mesh['grp'=4,'dev'=8] {'dev'}, dimensions={0}, use_global_device_ids=true | all-gather | bytes 276480 | tf_op jit(solution)/shard_map/all_gather | solution.py:47
  24.6 41.9 %while.34 = (s32[]{:T(128)}, f32[4,128]{1,0:T(4,128)S(1)}, s32[4]{0:T(128)}, s32[4,64]{1,0:T(4,128)S(1)}, f32[96,5,128]{2,1,0:T(8,128)S(1)}, /*index=5*/f32[4,1,...) while((s32[]{:T(128)}, f32[4,128]{1,0:T(4,128)S(1)}, ...), condition=%wide.region_3.4_spmd.clone.clone, body=%wide.region_0.3_spmd.sunk.clone.clone.sunk | while | flops 12065039 | bytes 4628909 | solution.py:71
  27.1 1.3 multiply_reduce_fusion.8
  28.4 1.4 multiply_reduce_fusion.9
  32.3 1.3 multiply_reduce_fusion.8
  33.7 1.4 multiply_reduce_fusion.9
  37.6 1.3 multiply_reduce_fusion.8
  38.9 1.4 multiply_reduce_fusion.9
  42.8 1.3 multiply_reduce_fusion.8
  44.1 1.4 multiply_reduce_fusion.9
  48.0 1.3 multiply_reduce_fusion.8
  49.4 1.4 multiply_reduce_fusion.9
  53.3 1.3 multiply_reduce_fusion.8
  54.6 1.4 multiply_reduce_fusion.9
  58.5 1.3 multiply_reduce_fusion.8
  59.9 1.4 multiply_reduce_fusion.9
  63.8 1.3 multiply_reduce_fusion.8
  65.1 1.4 multiply_reduce_fusion.9
  68.7 1.6 %collective-permute-done.3 = f32[4,128]{1,0:T(4,128)S(1)} collective-permute-done((f32[4,128]{1,0:T(4,128)S(1)}, f32[4,128]{1,0:T(4,128)S(1)}, u32[]{:S(2)}, u32[]{:S(2)}) %collective-permute-start.3) | collective-permute-done | bytes 2080 | tf_op jit(solution)/shard_map/ppermute | solution.py:21
  70.2 2.0 %collective-permute-done.2 = f32[4,128]{1,0:T(4,128)S(1)} collective-permute-done((f32[4,128]{1,0:T(4,128)S(1)}, f32[4,128]{1,0:T(4,128)S(1)}, u32[]{:S(2)}, u32[]{:S(2)}) %collective-permute-start.2) | collective-permute-done | bytes 2080 | tf_op jit(solution)/shard_map/ppermute | solution.py:18
  72.2 14.0 %all-gather = f32[8,12,128]{2,1,0:T(8,128)S(1)} all-gather(f32[1,12,128]{2,1,0:T(8,128)S(1)} %maximum_bitcast_fusion), channel_id=1, replica_groups=mesh['grp'=4,'dev'=8] {'dev'}, dimensions={0}, use_global_device_ids=true | all-gather | bytes 55296 | tf_op jit(solution)/shard_map/all_gather | solution.py:77
  86.2 61.1 %while.35 = (s32[]{:T(128)}, f32[4,3,128]{2,1,0:T(4,128)S(1)}, s32[4]{0:T(128)}, s32[4,64]{1,0:T(4,128)S(1)}, f32[96,5,128]{2,1,0:T(8,128)S(1)}, /*index=5*/f32[...) while((s32[]{:T(128)}, f32[4,3,128]{2,1,0:T(4,128)S(1)}, ...), condition=%wide.region_7.8_spmd.clone.clone, body=%wide.region_4.7_spmd.sunk.clone.clone.sunk | while | flops 21519628 | bytes 9044925 | solution.py:90
  89.3 1.3 multiply_reduce_fusion.10
  90.6 1.9 %fusion.24 = f32[4,8,128,128]{3,2,1,0:T(8,128)S(1)} fusion(f32[4,8,128,128]{3,2,1,0:T(8,128)S(1)} %multiply_reduce_fusion.10, f32[4,8,128]{2,1,0:T(8,128)S(1)} %bitcast.59, f32[4,8,128]{2,1,0:T(8,128)S(1)} %get-tuple-element.869, f32[4,8,128]{2,1,0:T(8,128)S(1)} %bitcast.60, f32[4,128]{1,0:T(4,128)S(1)} %bitcast.64, ...), kind=kLoop, calls=%fused_computation.25.clone.1 | loop fusion | flops 9437184 | bytes 4265984 | tf_op jit(solution)/shard_map/while/body/eval_jaxpr/mul | solution.py:84
  92.4 1.4 multiply_reduce_fusion.11
  96.9 1.3 multiply_reduce_fusion.10
  98.2 1.9 %fusion.24 = f32[4,8,128,128]{3,2,1,0:T(8,128)S(1)} fusion(f32[4,8,128,128]{3,2,1,0:T(8,128)S(1)} %multiply_reduce_fusion.10, f32[4,8,128]{2,1,0:T(8,128)S(1)} %bitcast.59, f32[4,8,128]{2,1,0:T(8,128)S(1)} %get-tuple-element.869, f32[4,8,128]{2,1,0:T(8,128)S(1)} %bitcast.60, f32[4,128]{1,0:T(4,128)S(1)} %bitcast.64, ...), kind=kLoop, calls=%fused_computation.25.clone.1 | loop fusion | flops 9437184 | bytes 4265984 | tf_op jit(solution)/shard_map/while/body/eval_jaxpr/mul | solution.py:84
  100.1 1.4 multiply_reduce_fusion.11
  104.5 1.3 multiply_reduce_fusion.10
  105.9 1.9 %fusion.24 = f32[4,8,128,128]{3,2,1,0:T(8,128)S(1)} fusion(f32[4,8,128,128]{3,2,1,0:T(8,128)S(1)} %multiply_reduce_fusion.10, f32[4,8,128]{2,1,0:T(8,128)S(1)} %bitcast.59, f32[4,8,128]{2,1,0:T(8,128)S(1)} %get-tuple-element.869, f32[4,8,128]{2,1,0:T(8,128)S(1)} %bitcast.60, f32[4,128]{1,0:T(4,128)S(1)} %bitcast.64, ...), kind=kLoop, calls=%fused_computation.25.clone.1 | loop fusion | flops 9437184 | bytes 4265984 | tf_op jit(solution)/shard_map/while/body/eval_jaxpr/mul | solution.py:84
  107.7 1.4 multiply_reduce_fusion.11
  112.2 1.3 multiply_reduce_fusion.10
  113.5 1.9 %fusion.24 = f32[4,8,128,128]{3,2,1,0:T(8,128)S(1)} fusion(f32[4,8,128,128]{3,2,1,0:T(8,128)S(1)} %multiply_reduce_fusion.10, f32[4,8,128]{2,1,0:T(8,128)S(1)} %bitcast.59, f32[4,8,128]{2,1,0:T(8,128)S(1)} %get-tuple-element.869, f32[4,8,128]{2,1,0:T(8,128)S(1)} %bitcast.60, f32[4,128]{1,0:T(4,128)S(1)} %bitcast.64, ...), kind=kLoop, calls=%fused_computation.25.clone.1 | loop fusion | flops 9437184 | bytes 4265984 | tf_op jit(solution)/shard_map/while/body/eval_jaxpr/mul | solution.py:84
  115.4 1.4 multiply_reduce_fusion.11
  119.8 1.3 multiply_reduce_fusion.10
  121.2 1.9 %fusion.24 = f32[4,8,128,128]{3,2,1,0:T(8,128)S(1)} fusion(f32[4,8,128,128]{3,2,1,0:T(8,128)S(1)} %multiply_reduce_fusion.10, f32[4,8,128]{2,1,0:T(8,128)S(1)} %bitcast.59, f32[4,8,128]{2,1,0:T(8,128)S(1)} %get-tuple-element.869, f32[4,8,128]{2,1,0:T(8,128)S(1)} %bitcast.60, f32[4,128]{1,0:T(4,128)S(1)} %bitcast.64, ...), kind=kLoop, calls=%fused_computation.25.clone.1 | loop fusion | flops 9437184 | bytes 4265984 | tf_op jit(solution)/shard_map/while/body/eval_jaxpr/mul | solution.py:84
  123.0 1.4 multiply_reduce_fusion.11
  127.5 1.3 multiply_reduce_fusion.10
  128.8 1.9 %fusion.24 = f32[4,8,128,128]{3,2,1,0:T(8,128)S(1)} fusion(f32[4,8,128,128]{3,2,1,0:T(8,128)S(1)} %multiply_reduce_fusion.10, f32[4,8,128]{2,1,0:T(8,128)S(1)} %bitcast.59, f32[4,8,128]{2,1,0:T(8,128)S(1)} %get-tuple-element.869, f32[4,8,128]{2,1,0:T(8,128)S(1)} %bitcast.60, f32[4,128]{1,0:T(4,128)S(1)} %bitcast.64, ...), kind=kLoop, calls=%fused_computation.25.clone.1 | loop fusion | flops 9437184 | bytes 4265984 | tf_op jit(solution)/shard_map/while/body/eval_jaxpr/mul | solution.py:84
  130.7 1.4 multiply_reduce_fusion.11
  135.1 1.3 multiply_reduce_fusion.10
  136.4 1.9 %fusion.24 = f32[4,8,128,128]{3,2,1,0:T(8,128)S(1)} fusion(f32[4,8,128,128]{3,2,1,0:T(8,128)S(1)} %multiply_reduce_fusion.10, f32[4,8,128]{2,1,0:T(8,128)S(1)} %bitcast.59, f32[4,8,128]{2,1,0:T(8,128)S(1)} %get-tuple-element.869, f32[4,8,128]{2,1,0:T(8,128)S(1)} %bitcast.60, f32[4,128]{1,0:T(4,128)S(1)} %bitcast.64, ...), kind=kLoop, calls=%fused_computation.25.clone.1 | loop fusion | flops 9437184 | bytes 4265984 | tf_op jit(solution)/shard_map/while/body/eval_jaxpr/mul | solution.py:84
  138.3 1.4 multiply_reduce_fusion.11
  142.7 1.3 multiply_reduce_fusion.10
  144.1 1.9 %fusion.24 = f32[4,8,128,128]{3,2,1,0:T(8,128)S(1)} fusion(f32[4,8,128,128]{3,2,1,0:T(8,128)S(1)} %multiply_reduce_fusion.10, f32[4,8,128]{2,1,0:T(8,128)S(1)} %bitcast.59, f32[4,8,128]{2,1,0:T(8,128)S(1)} %get-tuple-element.869, f32[4,8,128]{2,1,0:T(8,128)S(1)} %bitcast.60, f32[4,128]{1,0:T(4,128)S(1)} %bitcast.64, ...), kind=kLoop, calls=%fused_computation.25.clone.1 | loop fusion | flops 9437184 | bytes 4265984 | tf_op jit(solution)/shard_map/while/body/eval_jaxpr/mul | solution.py:84
  145.9 1.4 multiply_reduce_fusion.11
  (252 shorter events, 49.4 us)
Async XLA Ops:
  1.3 6.7 %collective-permute-start.1 = (f32[4,5,128]{2,1,0:T(8,128)S(1)}, f32[4,5,128]{2,1,0:T(8,128)S(1)}, u32[]{:S(2)}, u32[]{:S(2)}) collective-permute-start(f32[4,5,128]{2,1,0:T(8,128)S(1)} %copy.28), channel_id=1, source_target_pairs={{8,0},{16,8},{24,16},{0,24},{9,1},{17,9},{25,17},{1,25},{10,2},{18... | collective-permute-start | bytes 30728 | tf_op jit(solution)/shard_map/ppermute | solution.py:21
  5.3 4.6 %collective-permute-start = (f32[4,5,128]{2,1,0:T(8,128)S(1)}, f32[4,5,128]{2,1,0:T(8,128)S(1)}, u32[]{:S(2)}, u32[]{:S(2)}) collective-permute-start(f32[4,5,128]{2,1,0:T(8,128)S(1)} %copy.28), channel_id=1, source_target_pairs={{0,8},{8,16},{16,24},{24,0},{1,9},{9,17},{17,25},{25,1},{2,10},{10... | collective-permute-start | bytes 30728 | tf_op jit(solution)/shard_map/ppermute | solution.py:18
  24.6 41.9 %copy-start.1 = (f32[4,128]{1,0:T(4,128)S(1)}, f32[4,128]{1,0:T(4,128)}, u32[]{:S(2)}) copy-start(f32[4,128]{1,0:T(4,128)} %param.10) | copy-start | bytes 6148
  66.6 19.7 %copy-start = (f32[4,128]{1,0:T(4,128)}, f32[4,128]{1,0:T(4,128)S(1)}, u32[]{:S(2)}) copy-start(f32[4,128]{1,0:T(4,128)S(1)} %get-tuple-element.691) | copy-start | bytes 6148
  66.6 3.6 %collective-permute-start.3 = (f32[4,128]{1,0:T(4,128)S(1)}, f32[4,128]{1,0:T(4,128)S(1)}, u32[]{:S(2)}, u32[]{:S(2)}) collective-permute-start(f32[4,128]{1,0:T(4,128)S(1)} %multiply_divide_fusion), channel_id=1, source_target_pairs={{8,0},{16,8},{24,16},{0,24},{9,1},{17,9},{25,17},{1,25},{10,2},{18... | collective-permute-start | bytes 6152 | tf_op jit(solution)/shard_map/ppermute | solution.py:21
  67.7 4.5 %collective-permute-start.2 = (f32[4,128]{1,0:T(4,128)S(1)}, f32[4,128]{1,0:T(4,128)S(1)}, u32[]{:S(2)}, u32[]{:S(2)}) collective-permute-start(f32[4,128]{1,0:T(4,128)S(1)} %multiply_divide_fusion), channel_id=1, source_target_pairs={{0,8},{8,16},{16,24},{24,0},{1,9},{9,17},{17,25},{25,1},{2,10},{10... | collective-permute-start | bytes 6152 | tf_op jit(solution)/shard_map/ppermute | solution.py:18
where the time goes:
time: 149 us; the launch traced here: 148 us
  other arithmetic  86.7 us (58%)
  blocking collectives  28.7 us (19%)
  local copies, waits for them, and re-layouts  19.1 us (13%)
  starting transfers between devices  6 us (4%)
  waiting for transfers between devices  5.4 us (4%)
    reduce_sum x16, other arithmetic, fetch_block(): dist_sq = jnp.sum(offset * offset, axis=2)  21.1 us
    mul x8, other arithmetic, force_step(): live[:, :, None, None] * others[:, :, 3, None, :]  14.8 us
    all_gather x1, blocking collectives, on_device(): extended = lax.all_gather(rimmed, 'dev', axis=0, tiled=True)  14.7 us
    all_gather x1, blocking collectives, on_device(): weight_ext = lax.all_gather(weight_rim, 'dev', axis=0, tiled=True)  14 us
    mul x16, other arithmetic, fetch_block(): shift_blk[:, :, None, None, None] * unit_first[None, None, :, None, None]  11.7 us
    convert_element_type x16, other arithmetic, fetch_block(): ((block_at * NBLK + slot_range)[None, :] < counts[:, None]).astype(jnp.fl...  11.7 us
    reduce_sum x8, other arithmetic, density_step(): jnp.sum(live[:, :, None, None] * others[:, :, 3, None, :] * kernel, axis=...  11.5 us
    reduce_sum x8, other arithmetic, force_step(): return total - jnp.sum(factor[:, :, None] * offset, axis=(1, 4))  11.1 us
  transfers between devices with their start and end apart: 4, of which 3 were waited for; matrix products, arithmetic and copies ran while one was open for 2% of the time, Pallas kernels for 0%

commit v1 on v0

--- a/solution.py
+++ b/solution.py
@@ -44,7 +44,16 @@
     member_of = within // own_cells
     cell_of = within % own_cells
     rimmed = padded(particles, (("grp", 0),), own_cells)
-    extended = lax.all_gather(rimmed, "dev", axis=0, tiled=True)
+    value = rimmed
+    ways, here, turn = (lax.axis_size("dev"), lax.axis_index("dev"), value.shape[0])
+    lengths = [n * ways if d == 0 else n for d, n in enumerate(value.shape)]
+    full = lax.dynamic_update_slice_in_dim(
+        jnp.zeros(lengths, value.dtype), value, here * turn, axis=0
+    )
+    for far in range(1, ways):
+        value = lax.ppermute(value, "dev", [(d, (d + 1) % ways) for d in range(ways)])
+        full = lax.dynamic_update_slice_in_dim(full, value, (here - far) % ways * turn, axis=0)
+    extended = full
     slots_ext = member_of * (3 * own_cells) + side_of * own_cells + cell_of
     upper = NB // NBLK
     slot_range = jnp.arange(NBLK, dtype=jnp.int32)

time: 149 us -> 172 us (1.15)
  waiting for transfers between devices: 5.4 us -> 42.4 us
  blocking collectives: 28.7 us -> 14 us
    ppermute x0 -> x7, waiting for transfers between devices: none -> 37 us  [on_device(): lax.ppermute(value, 'dev', [(d, (d + 1) % ways) for d in range(ways)])]
    all_gather x1 -> x0, blocking collectives: 14.7 us -> none  [on_device(): extended = lax.all_gather(rimmed, 'dev', axis=0, tiled=True)]
  transfers between devices with their start and end apart: 4 -> 11, of which waited for: 3 -> 10; matrix products, arithmetic and copies ran while one was open for 2% -> 2% of each run, Pallas kernels for 0% -> 0%
where the time goes in v1:
time: 172 us; the launch traced here: 171 us
  other arithmetic  86.7 us (50%)
  waiting for transfers between devices  42.4 us (25%)
  local copies, waits for them, and re-layouts  19.9 us (12%)
  blocking collectives  14 us (8%)
  starting transfers between devices  6.02 us (4%)
    ppermute x7, waiting for transfers between devices, on_device(): lax.ppermute(value, 'dev', [(d, (d + 1) % ways) for d in range(ways)])  37 us
    reduce_sum x16, other arithmetic, fetch_block(): dist_sq = jnp.sum(offset * offset, axis=2)  21.1 us
    mul x8, other arithmetic, force_step(): live[:, :, None, None] * others[:, :, 3, None, :]  14.8 us
    all_gather x1, blocking collectives, on_device(): weight_ext = lax.all_gather(weight_rim, 'dev', axis=0, tiled=True)  14 us
    mul x16, other arithmetic, fetch_block(): shift_blk[:, :, None, None, None] * unit_first[None, None, :, None, None]  11.7 us
    convert_element_type x16, other arithmetic, fetch_block(): ((block_at * NBLK + slot_range)[None, :] < counts[:, None]).astype(jnp.fl...  11.6 us
    reduce_sum x8, other arithmetic, density_step(): jnp.sum(live[:, :, None, None] * others[:, :, 3, None, :] * kernel, axis=...  11.5 us
    reduce_sum x8, other arithmetic, force_step(): return total - jnp.sum(factor[:, :, None] * offset, axis=(1, 4))  11.1 us
  transfers between devices with their start and end apart: 11, of which 10 were waited for; matrix products, arithmetic and copies ran while one was open for 2% of the time, Pallas kernels for 0%

profile of v1, /device:TPU:0, one launch (start us, length us, event | category | flops | bytes accessed | tf_op | source)
XLA Modules:
  0.0 171.2 jit_solution(13830281718002956326)
XLA Ops:
  1.3 3.9 %collective-permute-start.1 = (f32[4,5,128]{2,1,0:T(8,128)S(1)}, f32[4,5,128]{2,1,0:T(8,128)S(1)}, u32[]{:S(2)}, u32[]{:S(2)}) collective-permute-start(f32[4,5,128]{2,1,0:T(8,128)S(1)} %copy.28), channel_id=1, source_target_pairs={{8,0},{16,8},{24,16},{0,24},{9,1},{17,9},{25,17},{1,25},{10,2},{18... | collective-permute-start | bytes 30728 | tf_op jit(solution)/shard_map/ppermute | solution.py:21
  8.0 1.9 %collective-permute-done = f32[4,5,128]{2,1,0:T(8,128)S(1)} collective-permute-done((f32[4,5,128]{2,1,0:T(8,128)S(1)}, f32[4,5,128]{2,1,0:T(8,128)S(1)}, u32[]{:S(2)}, u32[]{:S(2)}) %collective-permute-start) | collective-permute-done | bytes 10272 | tf_op jit(solution)/shard_map/ppermute | solution.py:18
  10.7 5.2 %collective-permute-done.2 = f32[12,5,128]{2,1,0:T(8,128)S(1)} collective-permute-done((f32[12,5,128]{2,1,0:T(8,128)S(1)}, f32[12,5,128]{2,1,0:T(8,128)S(1)}, u32[]{:S(2)}, u32[]{:S(2)}) %collective-permute-start.2) | collective-permute-done | bytes 30752 | tf_op jit(solution)/shard_map/ppermute | solution.py:54
  15.9 5.3 %collective-permute-done.3 = f32[12,5,128]{2,1,0:T(8,128)S(1)} collective-permute-done((f32[12,5,128]{2,1,0:T(8,128)S(1)}, f32[12,5,128]{2,1,0:T(8,128)S(1)}, u32[]{:S(2)}, u32[]{:S(2)}) %collective-permute-start.3) | collective-permute-done | bytes 30752 | tf_op jit(solution)/shard_map/ppermute | solution.py:54
  21.3 5.3 %collective-permute-done.4 = f32[12,5,128]{2,1,0:T(8,128)S(1)} collective-permute-done((f32[12,5,128]{2,1,0:T(8,128)S(1)}, f32[12,5,128]{2,1,0:T(8,128)S(1)}, u32[]{:S(2)}, u32[]{:S(2)}) %collective-permute-start.4) | collective-permute-done | bytes 30752 | tf_op jit(solution)/shard_map/ppermute | solution.py:54
  26.6 5.3 %collective-permute-done.5 = f32[12,5,128]{2,1,0:T(8,128)S(1)} collective-permute-done((f32[12,5,128]{2,1,0:T(8,128)S(1)}, f32[12,5,128]{2,1,0:T(8,128)S(1)}, u32[]{:S(2)}, u32[]{:S(2)}) %collective-permute-start.5) | collective-permute-done | bytes 30752 | tf_op jit(solution)/shard_map/ppermute | solution.py:54
  31.9 5.3 %collective-permute-done.6 = f32[12,5,128]{2,1,0:T(8,128)S(1)} collective-permute-done((f32[12,5,128]{2,1,0:T(8,128)S(1)}, f32[12,5,128]{2,1,0:T(8,128)S(1)}, u32[]{:S(2)}, u32[]{:S(2)}) %collective-permute-start.6) | collective-permute-done | bytes 30752 | tf_op jit(solution)/shard_map/ppermute | solution.py:54
  37.2 5.3 %collective-permute-done.7 = f32[12,5,128]{2,1,0:T(8,128)S(1)} collective-permute-done((f32[12,5,128]{2,1,0:T(8,128)S(1)}, f32[12,5,128]{2,1,0:T(8,128)S(1)}, u32[]{:S(2)}, u32[]{:S(2)}) %collective-permute-start.7) | collective-permute-done | bytes 30752 | tf_op jit(solution)/shard_map/ppermute | solution.py:54
  42.5 5.3 %collective-permute-done.8 = f32[12,5,128]{2,1,0:T(8,128)S(1)} collective-permute-done((f32[12,5,128]{2,1,0:T(8,128)S(1)}, f32[12,5,128]{2,1,0:T(8,128)S(1)}, u32[]{:S(2)}, u32[]{:S(2)}) %collective-permute-start.8) | collective-permute-done | bytes 30752 | tf_op jit(solution)/shard_map/ppermute | solution.py:54
  47.8 41.9 %while.34 = (s32[]{:T(128)}, f32[4,128]{1,0:T(4,128)S(1)}, s32[4]{0:T(128)}, s32[4,64]{1,0:T(4,128)S(1)}, f32[96,5,128]{2,1,0:T(8,128)S(1)}, /*index=5*/f32[4,1,...) while((s32[]{:T(128)}, f32[4,128]{1,0:T(4,128)S(1)}, ...), condition=%wide.region_3.4_spmd.clone.clone, body=%wide.region_0.3_spmd.sunk.clone.clone.sunk | while | flops 12065039 | bytes 4628909 | solution.py:80
  51.6 1.4 multiply_reduce_fusion.9
  55.5 1.3 multiply_reduce_fusion.8
  56.8 1.4 multiply_reduce_fusion.9
  62.1 1.4 multiply_reduce_fusion.9
  67.3 1.4 multiply_reduce_fusion.9
  72.6 1.4 multiply_reduce_fusion.9
  76.5 1.3 multiply_reduce_fusion.8
  77.8 1.4 multiply_reduce_fusion.9
  83.0 1.4 multiply_reduce_fusion.9
  88.3 1.4 multiply_reduce_fusion.9
  91.9 1.6 collective-permute-done.10
  93.4 2.0 %collective-permute-done.9 = f32[4,128]{1,0:T(4,128)S(1)} collective-permute-done((f32[4,128]{1,0:T(4,128)S(1)}, f32[4,128]{1,0:T(4,128)S(1)}, u32[]{:S(2)}, u32[]{:S(2)}) %collective-permute-start.9) | collective-permute-done | bytes 2080 | tf_op jit(solution)/shard_map/ppermute | solution.py:18
  95.4 14.0 %all-gather = f32[8,12,128]{2,1,0:T(8,128)S(1)} all-gather(f32[1,12,128]{2,1,0:T(8,128)S(1)} %maximum_bitcast_fusion), channel_id=1, replica_groups=mesh['grp'=4,'dev'=8] {'dev'}, dimensions={0}, use_global_device_ids=true | all-gather | bytes 55296 | tf_op jit(solution)/shard_map/all_gather | solution.py:86
  109.4 61.2 %while.35 = (s32[]{:T(128)}, f32[4,3,128]{2,1,0:T(4,128)S(1)}, s32[4]{0:T(128)}, s32[4,64]{1,0:T(4,128)S(1)}, f32[96,5,128]{2,1,0:T(8,128)S(1)}, /*index=5*/f32[...) while((s32[]{:T(128)}, f32[4,3,128]{2,1,0:T(4,128)S(1)}, ...), condition=%wide.region_7.8_spmd.clone.clone, body=%wide.region_4.7_spmd.sunk.clone.clone.sunk | while | flops 21519628 | bytes 9044925 | solution.py:99
  112.4 1.3 multiply_reduce_fusion.10
  113.8 1.9 %fusion.24 = f32[4,8,128,128]{3,2,1,0:T(8,128)S(1)} fusion(f32[4,8,128,128]{3,2,1,0:T(8,128)S(1)} %multiply_reduce_fusion.10, f32[4,8,128]{2,1,0:T(8,128)S(1)} %bitcast.59, f32[4,8,128]{2,1,0:T(8,128)S(1)} %get-tuple-element.869, f32[4,8,128]{2,1,0:T(8,128)S(1)} %bitcast.60, f32[4,128]{1,0:T(4,128)S(1)} %bitcast.64, ...), kind=kLoop, calls=%fused_computation.25.clone.1 | loop fusion | flops 9437184 | bytes 4265984 | tf_op jit(solution)/shard_map/while/body/eval_jaxpr/mul | solution.py:93
  115.6 1.4 multiply_reduce_fusion.11
  120.1 1.3 multiply_reduce_fusion.10
  121.4 1.9 %fusion.24 = f32[4,8,128,128]{3,2,1,0:T(8,128)S(1)} fusion(f32[4,8,128,128]{3,2,1,0:T(8,128)S(1)} %multiply_reduce_fusion.10, f32[4,8,128]{2,1,0:T(8,128)S(1)} %bitcast.59, f32[4,8,128]{2,1,0:T(8,128)S(1)} %get-tuple-element.869, f32[4,8,128]{2,1,0:T(8,128)S(1)} %bitcast.60, f32[4,128]{1,0:T(4,128)S(1)} %bitcast.64, ...), kind=kLoop, calls=%fused_computation.25.clone.1 | loop fusion | flops 9437184 | bytes 4265984 | tf_op jit(solution)/shard_map/while/body/eval_jaxpr/mul | solution.py:93
  123.3 1.4 multiply_reduce_fusion.11
  127.7 1.3 multiply_reduce_fusion.10
  129.1 1.9 %fusion.24 = f32[4,8,128,128]{3,2,1,0:T(8,128)S(1)} fusion(f32[4,8,128,128]{3,2,1,0:T(8,128)S(1)} %multiply_reduce_fusion.10, f32[4,8,128]{2,1,0:T(8,128)S(1)} %bitcast.59, f32[4,8,128]{2,1,0:T(8,128)S(1)} %get-tuple-element.869, f32[4,8,128]{2,1,0:T(8,128)S(1)} %bitcast.60, f32[4,128]{1,0:T(4,128)S(1)} %bitcast.64, ...), kind=kLoop, calls=%fused_computation.25.clone.1 | loop fusion | flops 9437184 | bytes 4265984 | tf_op jit(solution)/shard_map/while/body/eval_jaxpr/mul | solution.py:93
  130.9 1.4 multiply_reduce_fusion.11
  135.4 1.3 multiply_reduce_fusion.10
  136.7 1.9 %fusion.24 = f32[4,8,128,128]{3,2,1,0:T(8,128)S(1)} fusion(f32[4,8,128,128]{3,2,1,0:T(8,128)S(1)} %multiply_reduce_fusion.10, f32[4,8,128]{2,1,0:T(8,128)S(1)} %bitcast.59, f32[4,8,128]{2,1,0:T(8,128)S(1)} %get-tuple-element.869, f32[4,8,128]{2,1,0:T(8,128)S(1)} %bitcast.60, f32[4,128]{1,0:T(4,128)S(1)} %bitcast.64, ...), kind=kLoop, calls=%fused_computation.25.clone.1 | loop fusion | flops 9437184 | bytes 4265984 | tf_op jit(solution)/shard_map/while/body/eval_jaxpr/mul | solution.py:93
  138.6 1.4 multiply_reduce_fusion.11
  143.0 1.3 multiply_reduce_fusion.10
  144.3 1.9 %fusion.24 = f32[4,8,128,128]{3,2,1,0:T(8,128)S(1)} fusion(f32[4,8,128,128]{3,2,1,0:T(8,128)S(1)} %multiply_reduce_fusion.10, f32[4,8,128]{2,1,0:T(8,128)S(1)} %bitcast.59, f32[4,8,128]{2,1,0:T(8,128)S(1)} %get-tuple-element.869, f32[4,8,128]{2,1,0:T(8,128)S(1)} %bitcast.60, f32[4,128]{1,0:T(4,128)S(1)} %bitcast.64, ...), kind=kLoop, calls=%fused_computation.25.clone.1 | loop fusion | flops 9437184 | bytes 4265984 | tf_op jit(solution)/shard_map/while/body/eval_jaxpr/mul | solution.py:93
  146.2 1.4 multiply_reduce_fusion.11
  150.7 1.3 multiply_reduce_fusion.10
  152.0 1.9 %fusion.24 = f32[4,8,128,128]{3,2,1,0:T(8,128)S(1)} fusion(f32[4,8,128,128]{3,2,1,0:T(8,128)S(1)} %multiply_reduce_fusion.10, f32[4,8,128]{2,1,0:T(8,128)S(1)} %bitcast.59, f32[4,8,128]{2,1,0:T(8,128)S(1)} %get-tuple-element.869, f32[4,8,128]{2,1,0:T(8,128)S(1)} %bitcast.60, f32[4,128]{1,0:T(4,128)S(1)} %bitcast.64, ...), kind=kLoop, calls=%fused_computation.25.clone.1 | loop fusion | flops 9437184 | bytes 4265984 | tf_op jit(solution)/shard_map/while/body/eval_jaxpr/mul | solution.py:93
  153.8 1.4 multiply_reduce_fusion.11
  158.3 1.3 multiply_reduce_fusion.10
  159.6 1.9 %fusion.24 = f32[4,8,128,128]{3,2,1,0:T(8,128)S(1)} fusion(f32[4,8,128,128]{3,2,1,0:T(8,128)S(1)} %multiply_reduce_fusion.10, f32[4,8,128]{2,1,0:T(8,128)S(1)} %bitcast.59, f32[4,8,128]{2,1,0:T(8,128)S(1)} %get-tuple-element.869, f32[4,8,128]{2,1,0:T(8,128)S(1)} %bitcast.60, f32[4,128]{1,0:T(4,128)S(1)} %bitcast.64, ...), kind=kLoop, calls=%fused_computation.25.clone.1 | loop fusion | flops 9437184 | bytes 4265984 | tf_op jit(solution)/shard_map/while/body/eval_jaxpr/mul | solution.py:93
  161.5 1.4 multiply_reduce_fusion.11
  166.0 1.3 multiply_reduce_fusion.10
  167.3 1.9 %fusion.24 = f32[4,8,128,128]{3,2,1,0:T(8,128)S(1)} fusion(f32[4,8,128,128]{3,2,1,0:T(8,128)S(1)} %multiply_reduce_fusion.10, f32[4,8,128]{2,1,0:T(8,128)S(1)} %bitcast.59, f32[4,8,128]{2,1,0:T(8,128)S(1)} %get-tuple-element.869, f32[4,8,128]{2,1,0:T(8,128)S(1)} %bitcast.60, f32[4,128]{1,0:T(4,128)S(1)} %bitcast.64, ...), kind=kLoop, calls=%fused_computation.25.clone.1 | loop fusion | flops 9437184 | bytes 4265984 | tf_op jit(solution)/shard_map/while/body/eval_jaxpr/mul | solution.py:93
  169.1 1.4 multiply_reduce_fusion.11
  (276 shorter events, 58.1 us)
Async XLA Ops:
  1.3 9.3 %collective-permute-start.1 = (f32[4,5,128]{2,1,0:T(8,128)S(1)}, f32[4,5,128]{2,1,0:T(8,128)S(1)}, u32[]{:S(2)}, u32[]{:S(2)}) collective-permute-start(f32[4,5,128]{2,1,0:T(8,128)S(1)} %copy.28), channel_id=1, source_target_pairs={{8,0},{16,8},{24,16},{0,24},{9,1},{17,9},{25,17},{1,25},{10,2},{18... | collective-permute-start | bytes 30728 | tf_op jit(solution)/shard_map/ppermute | solution.py:21
  5.3 4.6 %collective-permute-start = (f32[4,5,128]{2,1,0:T(8,128)S(1)}, f32[4,5,128]{2,1,0:T(8,128)S(1)}, u32[]{:S(2)}, u32[]{:S(2)}) collective-permute-start(f32[4,5,128]{2,1,0:T(8,128)S(1)} %copy.28), channel_id=1, source_target_pairs={{0,8},{8,16},{16,24},{24,0},{1,9},{9,17},{17,25},{25,1},{2,10},{10... | collective-permute-start | bytes 30728 | tf_op jit(solution)/shard_map/ppermute | solution.py:18
  10.6 5.3 %collective-permute-start.2 = (f32[12,5,128]{2,1,0:T(8,128)S(1)}, f32[12,5,128]{2,1,0:T(8,128)S(1)}, u32[]{:S(2)}, u32[]{:S(2)}) collective-permute-start(f32[12,5,128]{2,1,0:T(8,128)S(1)} %constant_dynamic-update-slice_fusion), channel_id=1, source_target_pairs={{0,1},{1,2},{2,3},{3,4},{4,5},{5,6},{6,7},{7,0},{8,9},{9,10},{10,1... | collective-permute-start | bytes 92168 | tf_op jit(solution)/shard_map/ppermute | solution.py:54
  15.9 5.3 %collective-permute-start.3 = (f32[12,5,128]{2,1,0:T(8,128)S(1)}, f32[12,5,128]{2,1,0:T(8,128)S(1)}, u32[]{:S(2)}, u32[]{:S(2)}) collective-permute-start(f32[12,5,128]{2,1,0:T(8,128)S(1)} %collective-permute-done.2), channel_id=1, source_target_pairs={{0,1},{1,2},{2,3},{3,4},{4,5},{5,6},{6,7},{7,0},{8,9},{9,10},{10,1... | collective-permute-start | bytes 92168 | tf_op jit(solution)/shard_map/ppermute | solution.py:54
  21.2 5.3 %collective-permute-start.4 = (f32[12,5,128]{2,1,0:T(8,128)S(1)}, f32[12,5,128]{2,1,0:T(8,128)S(1)}, u32[]{:S(2)}, u32[]{:S(2)}) collective-permute-start(f32[12,5,128]{2,1,0:T(8,128)S(1)} %collective-permute-done.3), channel_id=1, source_target_pairs={{0,1},{1,2},{2,3},{3,4},{4,5},{5,6},{6,7},{7,0},{8,9},{9,10},{10,1... | collective-permute-start | bytes 92168 | tf_op jit(solution)/shard_map/ppermute | solution.py:54
  26.6 5.3 %collective-permute-start.5 = (f32[12,5,128]{2,1,0:T(8,128)S(1)}, f32[12,5,128]{2,1,0:T(8,128)S(1)}, u32[]{:S(2)}, u32[]{:S(2)}) collective-permute-start(f32[12,5,128]{2,1,0:T(8,128)S(1)} %collective-permute-done.4), channel_id=1, source_target_pairs={{0,1},{1,2},{2,3},{3,4},{4,5},{5,6},{6,7},{7,0},{8,9},{9,10},{10,1... | collective-permute-start | bytes 92168 | tf_op jit(solution)/shard_map/ppermute | solution.py:54
  31.9 5.3 %collective-permute-start.6 = (f32[12,5,128]{2,1,0:T(8,128)S(1)}, f32[12,5,128]{2,1,0:T(8,128)S(1)}, u32[]{:S(2)}, u32[]{:S(2)}) collective-permute-start(f32[12,5,128]{2,1,0:T(8,128)S(1)} %collective-permute-done.5), channel_id=1, source_target_pairs={{0,1},{1,2},{2,3},{3,4},{4,5},{5,6},{6,7},{7,0},{8,9},{9,10},{10,1... | collective-permute-start | bytes 92168 | tf_op jit(solution)/shard_map/ppermute | solution.py:54
  37.2 5.3 %collective-permute-start.7 = (f32[12,5,128]{2,1,0:T(8,128)S(1)}, f32[12,5,128]{2,1,0:T(8,128)S(1)}, u32[]{:S(2)}, u32[]{:S(2)}) collective-permute-start(f32[12,5,128]{2,1,0:T(8,128)S(1)} %collective-permute-done.6), channel_id=1, source_target_pairs={{0,1},{1,2},{2,3},{3,4},{4,5},{5,6},{6,7},{7,0},{8,9},{9,10},{10,1... | collective-permute-start | bytes 92168 | tf_op jit(solution)/shard_map/ppermute | solution.py:54
  42.5 5.3 %collective-permute-start.8 = (f32[12,5,128]{2,1,0:T(8,128)S(1)}, f32[12,5,128]{2,1,0:T(8,128)S(1)}, u32[]{:S(2)}, u32[]{:S(2)}) collective-permute-start(f32[12,5,128]{2,1,0:T(8,128)S(1)} %collective-permute-done.7), channel_id=1, source_target_pairs={{0,1},{1,2},{2,3},{3,4},{4,5},{5,6},{6,7},{7,0},{8,9},{9,10},{10,1... | collective-permute-start | bytes 92168 | tf_op jit(solution)/shard_map/ppermute | solution.py:54
  47.8 41.9 %copy-start.1 = (f32[4,128]{1,0:T(4,128)S(1)}, f32[4,128]{1,0:T(4,128)}, u32[]{:S(2)}) copy-start(f32[4,128]{1,0:T(4,128)} %param.10) | copy-start | bytes 6148
  89.7 19.6 %copy-start = (f32[4,128]{1,0:T(4,128)}, f32[4,128]{1,0:T(4,128)S(1)}, u32[]{:S(2)}) copy-start(f32[4,128]{1,0:T(4,128)S(1)} %get-tuple-element.691) | copy-start | bytes 6148
  89.8 3.6 %collective-permute-start.10 = (f32[4,128]{1,0:T(4,128)S(1)}, f32[4,128]{1,0:T(4,128)S(1)}, u32[]{:S(2)}, u32[]{:S(2)}) collective-permute-start(f32[4,128]{1,0:T(4,128)S(1)} %multiply_divide_fusion), channel_id=1, source_target_pairs={{8,0},{16,8},{24,16},{0,24},{9,1},{17,9},{25,17},{1,25},{10,2},{18... | collective-permute-start | bytes 6152 | tf_op jit(solution)/shard_map/ppermute | solution.py:21
  90.9 4.5 %collective-permute-start.9 = (f32[4,128]{1,0:T(4,128)S(1)}, f32[4,128]{1,0:T(4,128)S(1)}, u32[]{:S(2)}, u32[]{:S(2)}) collective-permute-start(f32[4,128]{1,0:T(4,128)S(1)} %multiply_divide_fusion), channel_id=1, source_target_pairs={{0,8},{8,16},{16,24},{24,0},{1,9},{9,17},{17,25},{25,1},{2,10},{10... | collective-permute-start | bytes 6152 | tf_op jit(solution)/shard_map/ppermute | solution.py:18
